TPU v7x, 32 devices: a whole 2x2x4 slice. The times are simulated.
32 devices in a mesh: prow: 8 (over z, y), pcol: 4 (over x, core).
Axes of the slice: x: 2, y: 2, z: 4, core: 2. Of those that a mesh axis runs over, the one named last changes fastest.
Arguments:
- a_panel: float32 [98304, 512], P('prow', 'pcol'), may hold values from -6 to 6
- u_rows: float32 [512, 98304], P('pcol', 'prow'), may hold values from -0.25 to 0.25
- u_col: float32 [98304, 2048], P('prow', 'pcol'), may hold values from -0.01953125 to 0.01953125
- c_in: float32 [98304, 2048], P('prow', 'pcol'), may hold values from -6 to 6
Outputs:
- c_out: float32 [98304, 2048], P('prow', 'pcol')
All inputs are finite; a program needn't handle non-finite values.
Results may differ from a plain program's by a relative error of at most 0.00007.
Values sent between devices are 32-bit elements; how exact they have to be, the bound alone decides.
A program may use at most 192 MiB of HBM per device.

v0:
```python
import jax
import jax.numpy as jnp
from jax import lax
from jax.sharding import PartitionSpec as P


def gather_later(u_rows):
    return lax.all_gather(u_rows, "pcol", axis=0, tiled=True)


def on_device(a_panel, u_rows, u_col, c_in):
    a_full = lax.all_gather(a_panel, "pcol", axis=1, tiled=True)
    partial_inner = jnp.dot(
        a_full.T, u_col, precision=lax.Precision.HIGHEST, preferred_element_type=jnp.float32
    )
    inner = lax.psum(partial_inner, "prow")
    u_full = gather_later(u_rows)
    result = c_in + jnp.dot(
        u_full.T, inner, precision=lax.Precision.HIGHEST, preferred_element_type=jnp.float32
    )
    return result


def solution(mesh):
    placed = (P("prow", "pcol"), P("pcol", "prow"), P("prow", "pcol"), P("prow", "pcol"))
    return jax.shard_map(
        on_device, mesh=mesh, in_specs=placed, out_specs=P("prow", "pcol"), check_vma=False
    )
```

profile of v0, /device:TPU:0, one launch (start us, length us, event | category | flops | bytes accessed | tf_op | source)
XLA Modules:
  0.0 486.4 jit_solution(6694891880605975887)
XLA Ops:
  6.5 0.0 all-gather.3.cloned.1.call-start
  6.5 0.7 all-gather.3.cloned.1.call-update
  7.3 0.0 all-gather.5.cloned.1.call-start
  7.3 0.7 all-gather.5.cloned.1.call-update
  8.0 0.0 all-reduce.2.cloned.1.call-start
  8.1 161.7 %all-gather.3.cloned.1.call-done = f32[12288,512]{1,0:T(8,128)} async-done(((f32[12288,128]{1,0:T(8,128)}), f32[12288,512]{1,0:T(8,128)}) %all-gather.3.cloned.1.call-update) | async-done | bytes 25165840 | tf_op jit(solution)/shard_map/all_gather | solution.py:12
  169.8 45.2 %fusion = f32[512,512]{1,0:T(8,128)} fusion(f32[12288,512]{1,0:T(8,128)} %all-gather.3.cloned.1.call-done, f32[12288,512]{1,0:T(8,128)} %param.6), kind=kOutput, calls=%fused_computation.1 | convolution fusion | flops 38654705664 | bytes 51380224 | tf_op jit(solution)/shard_map/dot_general | solution.py:13
  215.0 0.0 all-reduce.2.cloned.1.call-update
  215.0 24.7 %copy.5 = f32[12288,512]{0,1:T(8,128)} copy(f32[12288,512]{1,0:T(8,128)} %param.7) | data formatting | bytes 50331648 | tf_op args[3]
  239.7 86.5 %all-gather.5.cloned.1.call-done = f32[512,12288]{1,0:T(8,128)} async-done(((f32[128,12288]{1,0:T(8,128)}), f32[512,12288]{1,0:T(8,128)}) %all-gather.5.cloned.1.call-update) | async-done | bytes 25165840 | tf_op jit(solution)/shard_map/all_gather | solution.py:8
  326.2 81.8 %all-reduce.2.cloned.1.call-done = f32[512,512]{1,0:T(8,128)} async-done(((f32[512,512]{1,0:T(8,128)}), f32[512,512]{1,0:T(8,128)}) %all-reduce.2.cloned.1.call-update) | async-done | bytes 1048592 | tf_op jit(solution)/shard_map/psum | solution.py:16
  407.9 47.2 %bitcast_add_fusion = f32[12288,512]{0,1:T(8,128)} fusion(f32[12288,512]{0,1:T(8,128)} %copy.5, f32[512,512]{1,0:T(8,128)} %all-reduce.2.cloned.1.call-done, f32[512,12288]{1,0:T(8,128)} %all-gather.5.cloned.1.call-done), kind=kOutput, calls=%fused_computation | convolution fusion | flops 38660997120 | bytes 76546048 | tf_op jit(solution)/shard_map/dot_general | solution.py:18
  455.2 24.7 %copy.6 = f32[12288,512]{1,0:T(8,128)} copy(f32[12288,512]{0,1:T(8,128)} %bitcast_add_fusion) | data formatting | bytes 50331648 | tf_op jit(solution)/shard_map/add | solution.py:18
Async XLA Ops:
  6.5 163.3 %all-gather.3.cloned.1.call-start = ((), (), s32[]{:S(2)}) async-start(), calls=%async_computation | async-start | bytes 31457280 | tf_op jit(solution)/shard_map/all_gather | solution.py:12
  7.3 318.9 %all-gather.5.cloned.1.call-start = ((), (), s32[]{:S(2)}) async-start(), calls=%async_computation.2 | async-start | bytes 31457280 | tf_op jit(solution)/shard_map/all_gather | solution.py:8
  8.0 399.9 %all-reduce.2.cloned.1.call-start = ((), (), s32[]{:S(2)}) async-start(), calls=%async_computation.1 | async-start | bytes 2097152 | tf_op jit(solution)/shard_map/psum | solution.py:16
Sparse Core Ops, SparseCore 0:
  8.9 160.8 all-gather.2
  171.4 154.7 all-gather.4
  329.7 78.1 all-reduce.1
where the time goes:
time: 487 us; the launch traced here: 486 us
  waiting for transfers between devices  331 us (68%)
  matrix products  92.4 us (19%)
  local copies, waits for them, and re-layouts  49.4 us (10%)
  between operations  13.1 us (3%)
    all_gather x1, waiting for transfers between devices, on_device(): a_full = lax.all_gather(a_panel, 'pcol', axis=1, tiled=True)  162 us
    all_gather x1, waiting for transfers between devices, gather_later(): return lax.all_gather(u_rows, 'pcol', axis=0, tiled=True)  86.5 us
    psum x1, waiting for transfers between devices, on_device(): inner = lax.psum(partial_inner, 'prow')  81.8 us
    dot_general x1, matrix products, on_device(): jnp.dot(u_full.T, inner, precision=lax.Precision.HIGHEST, preferred_eleme...  47.2 us
    dot_general x1, matrix products, on_device(): jnp.dot(a_full.T, u_col, precision=lax.Precision.HIGHEST, preferred_eleme...  45.2 us
    unnamed x1, local copies, waits for them, and re-layouts  24.7 us
    add x1, local copies, waits for them, and re-layouts, on_device(): c_in + jnp.dot(u_full.T, inner, precision=lax.Precision.HIGHEST, preferre...  24.7 us
  transfers between devices with their start and end apart: 3, of which 3 were waited for; matrix products, arithmetic and copies ran while one was open for 14% of the time, Pallas kernels for 0%

commit v1 on v0

--- a/solution.py
+++ b/solution.py
@@ -13,7 +13,8 @@
     partial_inner = jnp.dot(
         a_full.T, u_col, precision=lax.Precision.HIGHEST, preferred_element_type=jnp.float32
     )
-    inner = lax.psum(partial_inner, "prow")
+    parts = lax.all_gather(partial_inner, "prow", axis=0, tiled=False)
+    inner = parts.sum(axis=0)
     u_full = gather_later(u_rows)
     result = c_in + jnp.dot(
         u_full.T, inner, precision=lax.Precision.HIGHEST, preferred_element_type=jnp.float32

time: 487 us -> 573 us (1.18)
  waiting for transfers between devices: 331 us -> 413 us
    all_gather x0 -> x1, waiting for transfers between devices: none -> 99 us  [on_device(): parts = lax.all_gather(partial_inner, 'prow', axis=0, tiled=False)]
    psum x1 -> x0, waiting for transfers between devices: 81.8 us -> none  [on_device(): inner = lax.psum(partial_inner, 'prow')]
    all_gather x1, waiting for transfers between devices: 86.5 us -> 150 us  [gather_later(): return lax.all_gather(u_rows, 'pcol', axis=0, tiled=True)]
  transfers between devices with their start and end apart: 3 -> 3, of which waited for: 3 -> 3; matrix products, arithmetic and copies ran while one was open for 14% -> 5% of each run, Pallas kernels for 0% -> 0%
where the time goes in v1:
time: 573 us; the launch traced here: 572 us
  waiting for transfers between devices  413 us (72%)
  matrix products  92.1 us (16%)
  local copies, waits for them, and re-layouts  49.6 us (9%)
  between operations  13.1 us (2%)
    all_gather x1, waiting for transfers between devices, on_device(): a_full = lax.all_gather(a_panel, 'pcol', axis=1, tiled=True)  162 us
    all_gather x1, waiting for transfers between devices, gather_later(): return lax.all_gather(u_rows, 'pcol', axis=0, tiled=True)  150 us
    all_gather x1, waiting for transfers between devices, on_device(): parts = lax.all_gather(partial_inner, 'prow', axis=0, tiled=False)  99 us
    dot_general x1, matrix products, on_device(): jnp.dot(u_full.T, inner, precision=lax.Precision.HIGHEST, preferred_eleme...  46.9 us
    dot_general x1, matrix products, on_device(): jnp.dot(a_full.T, u_col, precision=lax.Precision.HIGHEST, preferred_eleme...  45.2 us
    unnamed x1, local copies, waits for them, and re-layouts  24.9 us
    add x1, local copies, waits for them, and re-layouts, on_device(): c_in + jnp.dot(u_full.T, inner, precision=lax.Precision.HIGHEST, preferre...  24.7 us
  transfers between devices with their start and end apart: 3, of which 3 were waited for; matrix products, arithmetic and copies ran while one was open for 5% of the time, Pallas kernels for 0%

profile of v1, /device:TPU:0, one launch (start us, length us, event | category | flops | bytes accessed | tf_op | source)
XLA Modules:
  0.0 572.3 jit_solution(15801662190022713175)
XLA Ops:
  6.5 0.0 all-gather.5.cloned.1.call-start
  6.5 0.7 all-gather.5.cloned.1.call-update
  7.3 0.0 all-gather.9.cloned.1.call-start
  7.3 162.5 %all-gather.5.cloned.1.call-done = f32[12288,512]{1,0:T(8,128)} async-done(((f32[12288,128]{1,0:T(8,128)}), f32[12288,512]{1,0:T(8,128)}) %all-gather.5.cloned.1.call-update) | async-done | bytes 25165840 | tf_op jit(solution)/shard_map/all_gather | solution.py:12
  169.8 45.2 %fusion = f32[512,512]{1,0:T(8,128)} fusion(f32[12288,512]{1,0:T(8,128)} %all-gather.5.cloned.1.call-done, f32[12288,512]{1,0:T(8,128)} %param.6), kind=kOutput, calls=%fused_computation.1 | convolution fusion | flops 38654705664 | bytes 51380224 | tf_op jit(solution)/shard_map/dot_general | solution.py:13
  215.0 0.0 all-gather.9.cloned.1.call-update
  215.0 0.2 all-gather.7.cloned.1.call-start
  215.2 0.5 all-gather.7.cloned.1.call-update
  215.7 24.9 %copy.5 = f32[12288,512]{0,1:T(8,128)} copy(f32[12288,512]{1,0:T(8,128)} %param.7) | data formatting | bytes 50331648 | tf_op args[3]
  240.6 99.0 %all-gather.9.cloned.1.call-done = f32[4096,512]{1,0:T(8,128)} async-done(((f32[512,512]{1,0:T(8,128)}), f32[4096,512]{1,0:T(8,128)}) %all-gather.9.cloned.1.call-update) | async-done | bytes 8388624 | tf_op jit(solution)/shard_map/all_gather | solution.py:16
  339.6 4.5 reduce_sum.9
  344.1 150.1 %all-gather.7.cloned.1.call-done = f32[512,12288]{1,0:T(8,128)} async-done(((f32[128,12288]{1,0:T(8,128)}), f32[512,12288]{1,0:T(8,128)}) %all-gather.7.cloned.1.call-update) | async-done | bytes 25165840 | tf_op jit(solution)/shard_map/all_gather | solution.py:8
  494.2 46.9 %bitcast_add_fusion = f32[12288,512]{0,1:T(8,128)} fusion(f32[12288,512]{0,1:T(8,128)} %copy.5, f32[512,512]{1,0:T(8,128)S(1)} %reduce_sum.9, f32[512,12288]{1,0:T(8,128)} %all-gather.7.cloned.1.call-done), kind=kOutput, calls=%fused_computation | convolution fusion | flops 38660997120 | bytes 76546048 | tf_op jit(solution)/shard_map/dot_general | solution.py:19
  541.1 24.7 %copy.6 = f32[12288,512]{1,0:T(8,128)} copy(f32[12288,512]{0,1:T(8,128)} %bitcast_add_fusion) | data formatting | bytes 50331648 | tf_op jit(solution)/shard_map/add | solution.py:19
Async XLA Ops:
  6.5 163.3 %all-gather.5.cloned.1.call-start = ((), (), s32[]{:S(2)}) async-start(), calls=%async_computation | async-start | bytes 31457280 | tf_op jit(solution)/shard_map/all_gather | solution.py:12
  7.3 332.4 %all-gather.9.cloned.1.call-start = ((), (), s32[]{:S(2)}) async-start(), calls=%async_computation.2 | async-start | bytes 9437184 | tf_op jit(solution)/shard_map/all_gather | solution.py:16
  215.0 279.2 %all-gather.7.cloned.1.call-start = ((), (), s32[]{:S(2)}) async-start(), calls=%async_computation.1 | async-start | bytes 31457280 | tf_op jit(solution)/shard_map/all_gather | solution.py:8
Sparse Core Ops, SparseCore 0:
  8.9 160.8 all-gather.4
  215.1 124.4 all-gather.8
  341.2 152.9 all-gather.6
